TPU v7x, 128 devices: a whole 4x4x4 slice. The times are simulated.
128 devices in a mesh: group: 4 (over x), tile: 32 (over z, y, core).
Axes of the slice: x: 4, y: 4, z: 4, core: 2. Of those that a mesh axis runs over, the one named last changes fastest.
Arguments:
- frames: bfloat16 [12, 8, 128, 96, 256], P('group', None, 'tile'), may hold values from -6 to 6
- packing: int32 [12, 4], replicated, as said below
- w_space: bfloat16 [3, 3, 96, 96], replicated, may hold values from -0.21875 to 0.21875
- w_time: bfloat16 [3, 96, 96], replicated, may hold values from -0.375 to 0.375
- gain_one: float32 [96], replicated, may hold values from 0.1 to 1.9
- gain_two: float32 [96], replicated, may hold values from 0.1 to 1.9
Outputs:
- output: bfloat16 [12, 8, 128, 96, 256], P('group', None, 'tile')
Inputs may be any that keep to these rules, and one draw needn't show every extreme that they name: `packing`: column 0 is 1 where the slot's span continues a clip and 0 for a clip's first span, whose other source fields are not read. `packing`: a span with a successor has 8 valid frames, so every preceding span is full; the slots of one device have their preceding spans on distinct devices.
All inputs are finite; a program needn't handle non-finite values.
Results may differ from a plain program's by a relative error of at most 0.004.
Values may be sent and summed in bfloat16 or wider, within the bound.
No kernel may reach another device: no remote copies, remote signals or barrier semaphores. Data moves between devices by JAX's collectives and lax.ppermute only.
A program may use at most 192 MiB of HBM per device.

v0:
```python
import jax
import jax.numpy as jnp
from jax import lax
from jax.sharding import PartitionSpec as P


def extended_2(block, sides, width):
    for axis, dim in sides:
        count = lax.axis_size(axis)
        forward = [(i, i + 1) for i in range(count - 1)]
        backward = [(target, source) for source, target in forward]
        low = lax.ppermute(
            lax.slice_in_dim(block, block.shape[dim] - width, None, axis=dim), axis, forward
        )
        high = lax.ppermute(lax.slice_in_dim(block, 0, width, axis=dim), axis, backward)
        block = jnp.concatenate([low, block, high], axis=dim)
    return block


def norm_act(values, gain_vec):
    meansq = jnp.mean(values * values, axis=-2, keepdims=True)
    return jax.nn.silu(values * lax.rsqrt(meansq + 1e-06) * gain_vec[:, None])


def body(frames, packing, w_space, w_time, gain_one, gain_two):
    slot_count, frame_count, row_count, chan_count, col_count = frames.shape
    own_index = lax.axis_index("group")
    mine = lax.dynamic_slice_in_dim(packing, own_index * slot_count, slot_count, 0)
    hidden = norm_act(frames.astype(jnp.float32), gain_one).astype(jnp.bfloat16)
    rimmed = extended_2(hidden, (("tile", 2),), 1)
    padded = jnp.pad(rimmed, ((0, 0), (0, 0), (0, 0), (0, 0), (1, 1)))
    summed = jnp.zeros(frames.shape, jnp.float32)
    for tap_row in range(3):
        for tap_col in range(3):
            window = padded[:, :, tap_row : tap_row + row_count, :, tap_col : tap_col + col_count]
            summed = summed + jnp.einsum(
                "oi,nfyix->nfyox",
                w_space[tap_row, tap_col],
                window,
                preferred_element_type=jnp.float32,
            )
    act = norm_act(summed, gain_two).astype(jnp.bfloat16)
    tails = act[:, frame_count - 2 :]
    has_prev = mine[:, 0] > 0
    wanted = mine[:, 2] * slot_count + mine[:, 3]
    piece = lax.all_gather(tails, "group", axis=0, tiled=True)
    global_ids = jnp.arange(piece.shape[0], dtype=jnp.int32)
    select = ((wanted[:, None] == global_ids[None, :]) & has_prev[:, None]).astype(jnp.bfloat16)
    picked = jnp.einsum("sk,kfyix->sfyix", select, piece, preferred_element_type=jnp.float32)
    cache = picked.astype(jnp.bfloat16)
    extended = jnp.concatenate([cache, act], axis=1)
    temporal = jnp.zeros(frames.shape, jnp.float32)
    for tap in range(3):
        temporal = temporal + jnp.einsum(
            "oi,nfyix->nfyox",
            w_time[tap],
            extended[:, tap : tap + frame_count],
            preferred_element_type=jnp.float32,
        )
    keep = jnp.arange(frame_count, dtype=jnp.int32)[None, :] < mine[:, 1][:, None]
    result = jnp.where(keep[:, :, None, None, None], frames.astype(jnp.float32) + temporal, 0.0)
    return result.astype(jnp.bfloat16)


def solution(mesh):
    in_specs = (P("group", None, "tile", None, None), P(), P(), P(), P(), P())
    out_specs = P("group", None, "tile", None, None)
    return jax.shard_map(body, mesh=mesh, in_specs=in_specs, out_specs=out_specs, check_vma=False)
```

profile of v0, /device:TPU:1, one launch (start us, length us, event | category | flops | bytes accessed | tf_op | source)
XLA Modules:
  0.0 205.3 jit_solution(2057114716746689768)
XLA Ops:
  6.5 0.0 copy-start
  6.5 0.0 copy-start.3
  6.5 0.0 all-gather.2.cloned.1.call-start
  6.5 3.9 %fusion.6 = f32[3,8,4,256]{3,2,1,0:T(4,128)S(1)} fusion(bf16[3,8,4,96,256]{4,3,2,1,0:T(8,128)(2,1)} %param.6), kind=kLoop, calls=%fused_computation.11 | loop fusion | flops 7053312 | bytes 4816896 | tf_op jit(solution)/shard_map/reduce_sum | solution.py:21
  10.5 4.8 %fusion.13 = bf16[3,8,4,96,256]{4,3,2,1,0:T(8,128)(2,1)S(1)} fusion(bf16[3,8,4,96,256]{4,3,2,1,0:T(8,128)(2,1)} %param.6, f32[96]{0:T(128)} %param.10, f32[3,8,4,256]{3,2,1,0:T(4,128)S(1)} %add_rsqrt_fusion.1), kind=kLoop, calls=%fused_computation.18 | loop fusion | flops 18874368 | bytes 9535872 | tf_op jit(solution)/shard_map/convert_element_type | solution.py:29
  15.3 0.2 fusion.80
  15.5 4.6 %collective-permute-start = (bf16[3,8,1,96,256]{4,3,2,1,0:T(8,128)(2,1)S(1)}, bf16[3,8,1,96,256]{4,3,2,1,0:T(8,128)(2,1)S(1)}, u32[]{:S(2)}, u32[]{:S(2)}) collective-permute-start(bf16[3,8,1,96,256]{4,3,2,1,0:T(8,128)(2,1)S(1)} %get-tuple-element.5), channel_id=1, source_target_pairs={{0,1},{1,2},{2,3},{3,4},{4,5},{5,6},{6,7},{7,8},{8,9},{9,10},{10,1... | collective-permute-start | bytes 3538952 | tf_op jit(solution)/shard_map/ppermute | solution.py:12
  20.1 2.1 %collective-permute-start.1 = (bf16[3,8,1,96,256]{4,3,2,1,0:T(8,128)(2,1)S(1)}, bf16[3,8,1,96,256]{4,3,2,1,0:T(8,128)(2,1)S(1)}, u32[]{:S(2)}, u32[]{:S(2)}) collective-permute-start(bf16[3,8,1,96,256]{4,3,2,1,0:T(8,128)(2,1)S(1)} %get-tuple-element.6), channel_id=1, source_target_pairs={{1,0},{2,1},{3,2},{4,3},{5,4},{6,5},{7,6},{8,7},{9,8},{10,9},{11,1... | collective-permute-start | bytes 3538952 | tf_op jit(solution)/shard_map/ppermute | solution.py:15
  22.2 0.0 copy-done.3
  22.2 5.0 %fusion.53 = f32[3,8,4,256,96]{3,4,2,1,0:T(8,128)} fusion(bf16[3,8,4,96,256]{4,3,2,1,0:T(8,128)(2,1)S(1)} %fusion.13, bf16[3,3,96,96]{3,2,1,0:T(8,128)(2,1)S(1)} %copy-done.3), kind=kOutput, calls=%fused_computation.67 | convolution fusion | flops 452984832 | bytes 14180352 | tf_op jit(solution)/shard_map/oi,nfyix->nfyox/dot_general | solution.py:36
  27.3 6.0 %collective-permute-done = bf16[3,8,1,96,256]{4,3,2,1,0:T(8,128)(2,1)S(1)} collective-permute-done((bf16[3,8,1,96,256]{4,3,2,1,0:T(8,128)(2,1)S(1)}, bf16[3,8,1,96,256]{4,3,2,1,0:T(8,128)(2,1)S(1)}, u32[]{:S(2)}, u32[]{:S(2)}) %collective-permute-start) | collective-permute-done | bytes 1179680 | tf_op jit(solution)/shard_map/ppermute | solution.py:12
  33.2 4.4 %collective-permute-done.1 = bf16[3,8,1,96,256]{4,3,2,1,0:T(8,128)(2,1)S(1)} collective-permute-done((bf16[3,8,1,96,256]{4,3,2,1,0:T(8,128)(2,1)S(1)}, bf16[3,8,1,96,256]{4,3,2,1,0:T(8,128)(2,1)S(1)}, u32[]{:S(2)}, u32[]{:S(2)}) %collective-permute-start.1) | collective-permute-done | bytes 1179680 | tf_op jit(solution)/shard_map/ppermute | solution.py:15
  37.6 7.1 %fusion.5 = bf16[3,8,6,96,258]{4,3,2,1,0:T(8,128)(2,1)S(1)} fusion(bf16[3,8,1,96,256]{4,3,2,1,0:T(8,128)(2,1)S(1)} %collective-permute-done.1, bf16[3,8,4,96,256]{4,3,2,1,0:T(8,128)(2,1)S(1)} %fusion.13, bf16[3,8,1,96,256]{4,3,2,1,0:T(8,128)(2,1)S(1)} %collective-permute-done), kind=kLoop, calls=%fused_computation.10 | loop fusion | flops 42799104 | bytes 14211072 | tf_op jit(solution)/shard_map/concatenate | solution.py:16
  44.7 0.0 copy-start.1
  44.7 5.5 %fusion.31 = f32[3,8,4,256,96]{3,4,2,1,0:T(8,128)} fusion(bf16[3,8,6,96,258]{4,3,2,1,0:T(8,128)(2,1)S(1)} %fusion.5, bf16[3,3,96,96]{3,2,1,0:T(8,128)(2,1)S(1)} %copy-done.3), kind=kOutput, calls=%fused_computation.43 | convolution fusion | flops 452984832 | bytes 14180352 | tf_op jit(solution)/shard_map/oi,nfyix->nfyox/dot_general | solution.py:36
  50.2 5.2 %fusion.33 = f32[3,8,4,256,96]{3,4,2,1,0:T(8,128)} fusion(bf16[3,8,6,96,258]{4,3,2,1,0:T(8,128)(2,1)S(1)} %fusion.5, bf16[3,3,96,96]{3,2,1,0:T(8,128)(2,1)S(1)} %copy-done.3), kind=kOutput, calls=%fused_computation.45 | convolution fusion | flops 452984832 | bytes 14180352 | tf_op jit(solution)/shard_map/oi,nfyix->nfyox/dot_general | solution.py:36
  55.3 5.1 %fusion.35 = f32[3,8,4,256,96]{3,4,2,1,0:T(8,128)} fusion(bf16[3,8,6,96,258]{4,3,2,1,0:T(8,128)(2,1)S(1)} %fusion.5, bf16[3,3,96,96]{3,2,1,0:T(8,128)(2,1)S(1)} %copy-done.3), kind=kOutput, calls=%fused_computation.47 | convolution fusion | flops 452984832 | bytes 14180352 | tf_op jit(solution)/shard_map/oi,nfyix->nfyox/dot_general | solution.py:36
  60.4 5.1 %fusion.37 = f32[3,8,4,256,96]{3,4,2,1,0:T(8,128)} fusion(bf16[3,8,6,96,258]{4,3,2,1,0:T(8,128)(2,1)S(1)} %fusion.5, bf16[3,3,96,96]{3,2,1,0:T(8,128)(2,1)S(1)} %copy-done.3), kind=kOutput, calls=%fused_computation.49 | convolution fusion | flops 452984832 | bytes 14180352 | tf_op jit(solution)/shard_map/oi,nfyix->nfyox/dot_general | solution.py:36
  65.5 0.0 copy-done.1
  65.5 4.9 %fusion.41 = f32[3,8,4,256,96]{3,4,2,1,0:T(8,128)} fusion(bf16[3,8,6,96,258]{4,3,2,1,0:T(8,128)(2,1)S(1)} %fusion.5, bf16[3,3,96,96]{3,2,1,0:T(8,128)(2,1)S(1)} %copy-done.3), kind=kOutput, calls=%fused_computation.54 | convolution fusion | flops 452984832 | bytes 14180352 | tf_op jit(solution)/shard_map/oi,nfyix->nfyox/dot_general | solution.py:36
  70.5 5.1 %fusion.29 = f32[3,8,4,256,96]{3,4,2,1,0:T(8,128)} fusion(bf16[3,8,1,96,256]{4,3,2,1,0:T(8,128)(2,1)S(1)} %collective-permute-done.1, bf16[3,8,4,96,256]{4,3,2,1,0:T(8,128)(2,1)S(1)} %fusion.13, bf16[3,3,96,96]{3,2,1,0:T(8,128)(2,1)S(1)} %copy-done.3), kind=kOutput, calls=%fused_computation.41 | convolution fusion | flops 462422016 | bytes 15360000 | tf_op jit(solution)/shard_map/oi,nfyix->nfyox/dot_general | solution.py:36
  75.6 4.4 %fusion.39 = f32[3,8,4,256,96]{3,4,2,1,0:T(8,128)} fusion(bf16[3,8,4,96,256]{4,3,2,1,0:T(8,128)(2,1)S(1)} %fusion.13, bf16[3,8,1,96,256]{4,3,2,1,0:T(8,128)(2,1)S(1)} %collective-permute-done, bf16[3,3,96,96]{3,2,1,0:T(8,128)(2,1)S(1)} %copy-done.3), kind=kOutput, calls=%fused_computation.52 | convolution fusion | flops 462422016 | bytes 15360000 | tf_op jit(solution)/shard_map/oi,nfyix->nfyox/dot_general | solution.py:36
  80.0 0.0 copy-start.5
  80.0 31.7 %multiply_reduce_fusion = (f32[3,8,4,256]{3,2,1,0:T(4,128)S(1)}, f32[3,8,4,256,96]{3,4,2,1,0:T(8,128)}) fusion(bf16[3,8,6,96,258]{4,3,2,1,0:T(8,128)(2,1)} %copy-done.1, bf16[3,3,96,96]{3,2,1,0:T(8,128)(2,1)S(1)} %copy-done.3, f32[3,8,4,256,96]{3,4,2,1,0:T(8,128)} %fusion.29, f32[3,8,4,256,96]{3,4,2,1,0:T(8,128)} %fusion.31, ...), kind=kOutput, calls=%fused_computation.26 | convolution fusion | flops 476553216 | bytes 89776128 | tf_op jit(solution)/shard_map/oi,nfyix->nfyox/dot_general | solution.py:36
  111.7 0.0 copy-start.4
  111.8 0.0 copy-done.5
  111.8 5.8 %fusion.19 = bf16[3,8,4,96,256]{4,3,2,1,0:T(8,128)(2,1)S(1)} fusion(f32[3,8,4,256,96]{3,4,2,1,0:T(8,128)} %get-tuple-element.10, f32[96]{0:T(128)S(1)} %copy-done.5, f32[3,8,4,256]{3,2,1,0:T(4,128)S(1)} %add_rsqrt_fusion), kind=kLoop, calls=%fused_computation.28 | loop fusion | flops 16515072 | bytes 14254464 | tf_op jit(solution)/shard_map/convert_element_type | solution.py:42
  117.6 0.0 copy-start.2
  117.6 2.2 %copy-done.2 = bf16[3,8,4,96,256]{4,3,2,1,0:T(8,128)(2,1)} copy-done((bf16[3,8,4,96,256]{4,3,2,1,0:T(8,128)(2,1)}, bf16[3,8,4,96,256]{4,3,2,1,0:T(8,128)(2,1)S(1)}, u32[]{:S(2)}) %copy-start.2) | copy-done | bytes 4718616
  119.7 1.1 slice.133
  120.8 0.0 all-gather.2.cloned.1.call-update
  120.9 0.0 copy-done
  120.9 0.1 constant_dynamic-slice_fusion
  121.0 0.1 iota_compare_fusion.3
  121.0 0.0 copy-done.4
  121.0 7.4 %fusion.45 = f32[3,8,4,256,96]{3,4,2,1,0:T(8,128)} fusion(bf16[3,8,4,96,256]{4,3,2,1,0:T(8,128)(2,1)} %copy-done.2, bf16[3,96,96]{2,1,0:T(8,128)(2,1)S(1)} %copy-done.4), kind=kOutput, calls=%fused_computation.59 | convolution fusion | flops 452984832 | bytes 14180352 | tf_op jit(solution)/shard_map/oi,nfyix->nfyox/dot_general | solution.py:54
  128.4 0.0 slice-start
  128.4 48.3 %all-gather.2.cloned.1.call-done = bf16[12,2,4,96,256]{4,3,2,1,0:T(8,128)(2,1)} async-done(((bf16[3,2,4,96,256]{4,3,2,1,0:T(8,128)(2,1)}), bf16[12,2,4,96,256]{4,3,2,1,0:T(8,128)(2,1)}) %all-gather.2.cloned.1.call-update) | async-done | bytes 4718608 | tf_op jit(solution)/shard_map/all_gather | solution.py:46
  176.7 0.0 slice-start.1
  176.7 5.4 %fusion.20 = bf16[3,2,4,96,256]{4,0,3,2,1:T(4,128)(2,1)S(1)} fusion(bf16[12,2,4,96,256]{4,3,2,1,0:T(8,128)(2,1)} %all-gather.2.cloned.1.call-done, s32[3]{0:T(128)S(1)} %get-tuple-element.8, pred[3]{0:T(512)(128)(4,1)S(1)} %compare_bitcast_fusion), kind=kOutput, calls=%fused_computation.29 | convolution fusion | flops 14155848 | bytes 5898255 | tf_op jit(solution)/shard_map/sk,kfyix->sfyix/dot_general | solution.py:49
  182.1 0.2 copy.27
  182.3 0.0 slice-done
  182.3 0.0 slice-done.1
  182.4 4.4 %fusion.23 = f32[3,8,4,256,96]{3,4,2,1,0:T(8,128)} fusion(bf16[3,2,4,96,256]{4,3,2,1,0:T(8,128)(2,1)S(1)} %copy.27, bf16[3,8,4,96,256]{4,3,2,1,0:T(8,128)(2,1)S(1)} %bitcast.115, bf16[3,96,96]{2,1,0:T(8,128)(2,1)S(1)} %copy-done.4), kind=kOutput, calls=%fused_computation.34 | convolution fusion | flops 462422016 | bytes 15360000 | tf_op jit(solution)/shard_map/oi,nfyix->nfyox/dot_general | solution.py:54
  186.8 11.7 %fusion.15 = bf16[3,8,4,96,256]{4,3,2,1,0:T(8,128)(2,1)} fusion(bf16[3,8,4,96,256]{4,3,2,1,0:T(8,128)(2,1)} %param.6, f32[3,8,4,256,96]{3,4,2,1,0:T(8,128)} %fusion.45, f32[3,8,4,256,96]{3,4,2,1,0:T(8,128)} %fusion.23, pred[3,8]{1,0:T(4,128)(4,1)S(1)} %iota_compare_fusion.3, bf16[3,8,4,96,256]{4,3,2,1,0:T(8,128)(2,1)S(1)} %bitcast.115, ...), kind=kOutput, calls=%fused_computation.20 | convolution fusion | flops 476577792 | bytes 34234880 | tf_op jit(solution)/shard_map/oi,nfyix->nfyox/dot_general | solution.py:54
  (5 shorter events, 0.1 us)
Async XLA Ops:
  6.5 114.3 %copy-start = (s32[12,4]{0,1:T(4,128)S(1)}, s32[12,4]{0,1:T(4,128)}, u32[]{:S(2)}) copy-start(s32[12,4]{0,1:T(4,128)} %param.7) | copy-start | bytes 580
  6.5 15.7 %copy-start.3 = (bf16[3,3,96,96]{3,2,1,0:T(8,128)(2,1)S(1)}, bf16[3,3,96,96]{3,2,1,0:T(8,128)(2,1)}, u32[]{:S(2)}) copy-start(bf16[3,3,96,96]{3,2,1,0:T(8,128)(2,1)} %param.8) | copy-start | bytes 497668
  6.5 170.2 %all-gather.2.cloned.1.call-start = ((), (), s32[]{:S(2)}) async-start(), calls=%async_computation | async-start | bytes 5898240 | tf_op jit(solution)/shard_map/all_gather | solution.py:46
  15.5 17.7 %collective-permute-start = (bf16[3,8,1,96,256]{4,3,2,1,0:T(8,128)(2,1)S(1)}, bf16[3,8,1,96,256]{4,3,2,1,0:T(8,128)(2,1)S(1)}, u32[]{:S(2)}, u32[]{:S(2)}) collective-permute-start(bf16[3,8,1,96,256]{4,3,2,1,0:T(8,128)(2,1)S(1)} %get-tuple-element.5), channel_id=1, source_target_pairs={{0,1},{1,2},{2,3},{3,4},{4,5},{5,6},{6,7},{7,8},{8,9},{9,10},{10,1... | collective-permute-start | bytes 3538952 | tf_op jit(solution)/shard_map/ppermute | solution.py:12
  20.1 17.5 %collective-permute-start.1 = (bf16[3,8,1,96,256]{4,3,2,1,0:T(8,128)(2,1)S(1)}, bf16[3,8,1,96,256]{4,3,2,1,0:T(8,128)(2,1)S(1)}, u32[]{:S(2)}, u32[]{:S(2)}) collective-permute-start(bf16[3,8,1,96,256]{4,3,2,1,0:T(8,128)(2,1)S(1)} %get-tuple-element.6), channel_id=1, source_target_pairs={{1,0},{2,1},{3,2},{4,3},{5,4},{6,5},{7,6},{8,7},{9,8},{10,9},{11,1... | collective-permute-start | bytes 3538952 | tf_op jit(solution)/shard_map/ppermute | solution.py:15
  44.7 20.8 %copy-start.1 = (bf16[3,8,6,96,258]{4,3,2,1,0:T(8,128)(2,1)}, bf16[3,8,6,96,258]{4,3,2,1,0:T(8,128)(2,1)S(1)}, u32[]{:S(2)}) copy-start(bf16[3,8,6,96,258]{4,3,2,1,0:T(8,128)(2,1)S(1)} %fusion.5) | copy-start | bytes 21399556
  80.0 31.8 %copy-start.5 = (f32[96]{0:T(128)S(1)}, f32[96]{0:T(128)}, u32[]{:S(2)}) copy-start(f32[96]{0:T(128)} %param.11) | copy-start | bytes 1156
  111.7 9.4 %copy-start.4 = (bf16[3,96,96]{2,1,0:T(8,128)(2,1)S(1)}, bf16[3,96,96]{2,1,0:T(8,128)(2,1)}, u32[]{:S(2)}) copy-start(bf16[3,96,96]{2,1,0:T(8,128)(2,1)} %param.9) | copy-start | bytes 165892
  117.6 2.2 %copy-start.2 = (bf16[3,8,4,96,256]{4,3,2,1,0:T(8,128)(2,1)}, bf16[3,8,4,96,256]{4,3,2,1,0:T(8,128)(2,1)S(1)}, u32[]{:S(2)}) copy-start(bf16[3,8,4,96,256]{4,3,2,1,0:T(8,128)(2,1)S(1)} %fusion.19) | copy-start | bytes 14155780
  128.4 53.9 %slice-start = ((s8[4718592]{0:T(1024)(128)(4,1)}), s8[524288]{0:T(1024)(128)(4,1)S(1)}, s32[]{:S(2)}) async-start(s8[4718592]{0:T(1024)(128)(4,1)} %bitcast.114), calls=%async_computation.1 | async-start | bytes 1048576
  176.7 5.6 %slice-start.1 = ((s8[4718592]{0:T(1024)(128)(4,1)}), s8[4194304]{0:T(1024)(128)(4,1)S(1)}, s32[]{:S(2)}) async-start(s8[4718592]{0:T(1024)(128)(4,1)} %bitcast.114), calls=%async_computation.2 | async-start | bytes 8388608
Sparse Core Ops, SparseCore 0:
  121.0 55.6 all-gather.1
where the time goes:
time: 205 us
  matrix products  101 us (49%)
  waiting for transfers between devices  58.7 us (29%)
  other arithmetic  21.8 us (11%)
  between operations  13.6 us (7%)
  starting transfers between devices  6.69 us (3%)
  local copies, waits for them, and re-layouts  3.75 us (2%)
    dot_general x9, matrix products, body(): jnp.einsum('oi,nfyix->nfyox', w_space[tap_row, tap_col], window, preferre...  72 us
    all_gather x1, waiting for transfers between devices, body(): piece = lax.all_gather(tails, 'group', axis=0, tiled=True)  48.3 us
    dot_general x3, matrix products, body(): jnp.einsum('oi,nfyix->nfyox', w_time[tap], extended[:, tap:tap + frame_co...  23.5 us
    concatenate x1, other arithmetic, extended_2(): block = jnp.concatenate([low, block, high], axis=dim)  7.08 us
    ppermute x1, waiting for transfers between devices, extended_2(): lax.ppermute(lax.slice_in_dim(block, block.shape[dim] - width, None, axis...  5.96 us
    convert_element_type x1, other arithmetic, body(): act = norm_act(summed, gain_two).astype(jnp.bfloat16)  5.78 us
    dot_general x1, matrix products, body(): jnp.einsum('sk,kfyix->sfyix', select, piece, preferred_element_type=jnp.f...  5.4 us
    convert_element_type x1, other arithmetic, body(): hidden = norm_act(frames.astype(jnp.float32), gain_one).astype(jnp.bfloat16)  4.83 us
  transfers between devices with their start and end apart: 3, of which 3 were waited for; matrix products, arithmetic and copies ran while one was open for 6% of the time, Pallas kernels for 0%

commit v1 on v0

--- a/solution.py
+++ b/solution.py
@@ -43,7 +43,9 @@
     tails = act[:, frame_count - 2 :]
     has_prev = mine[:, 0] > 0
     wanted = mine[:, 2] * slot_count + mine[:, 3]
-    piece = lax.all_gather(tails, "group", axis=0, tiled=True)
+    piece = jnp.concatenate(
+        lax.all_to_all(jnp.stack([tails] * lax.axis_size("group")), "group", 0, 0), axis=0
+    )
     global_ids = jnp.arange(piece.shape[0], dtype=jnp.int32)
     select = ((wanted[:, None] == global_ids[None, :]) & has_prev[:, None]).astype(jnp.bfloat16)
     picked = jnp.einsum("sk,kfyix->sfyix", select, piece, preferred_element_type=jnp.float32)

time: 205 us -> 197 us (0.961)
  the two profiles are of different devices: /device:TPU:1 before, /device:TPU:64 now
where the time goes in v1:
time: 197 us
  matrix products  101 us (51%)
  waiting for transfers between devices  55.6 us (28%)
  other arithmetic  21.8 us (11%)
  starting transfers between devices  12.8 us (6%)
  local copies, waits for them, and re-layouts  5.46 us (3%)
    dot_general x9, matrix products, body(): jnp.einsum('oi,nfyix->nfyox', w_space[tap_row, tap_col], window, preferre...  71.9 us
    all_to_all x1, waiting for transfers between devices, body(): lax.all_to_all(jnp.stack([tails] * lax.axis_size('group')), 'group', 0, 0)  47.1 us
    dot_general x3, matrix products, body(): jnp.einsum('oi,nfyix->nfyox', w_time[tap], extended[:, tap:tap + frame_co...  23.5 us
    concatenate x1, other arithmetic, extended_2(): block = jnp.concatenate([low, block, high], axis=dim)  7.08 us
    ppermute x1, waiting for transfers between devices, extended_2(): lax.ppermute(lax.slice_in_dim(block, block.shape[dim] - width, None, axis...  6.7 us
    ppermute x1, starting transfers between devices, extended_2(): lax.ppermute(lax.slice_in_dim(block, 0, width, axis=dim), axis, backward)  5.93 us
    convert_element_type x1, other arithmetic, body(): act = norm_act(summed, gain_two).astype(jnp.bfloat16)  5.78 us
    dot_general x1, matrix products, body(): jnp.einsum('sk,kfyix->sfyix', select, piece, preferred_element_type=jnp.f...  5.4 us
  transfers between devices with their start and end apart: 3, of which 3 were waited for; matrix products, arithmetic and copies ran while one was open for 6% of the time, Pallas kernels for 0%

profile of v1, /device:TPU:64, one launch (start us, length us, event | category | flops | bytes accessed | tf_op | source)
XLA Modules:
  0.0 196.6 jit_solution(12665773499144607125)
XLA Ops:
  0.0 0.0 copy-start
  0.0 0.0 copy-start.3
  0.0 3.9 %fusion.6 = f32[3,8,4,256]{3,2,1,0:T(4,128)S(1)} fusion(bf16[3,8,4,96,256]{4,3,2,1,0:T(8,128)(2,1)} %param.6), kind=kLoop, calls=%fused_computation.11 | loop fusion | flops 7053312 | bytes 4816896 | tf_op jit(solution)/shard_map/reduce_sum | solution.py:21
  4.0 4.8 %fusion.13 = bf16[3,8,4,96,256]{4,3,2,1,0:T(8,128)(2,1)S(1)} fusion(bf16[3,8,4,96,256]{4,3,2,1,0:T(8,128)(2,1)} %param.6, f32[96]{0:T(128)} %param.10, f32[3,8,4,256]{3,2,1,0:T(4,128)S(1)} %add_rsqrt_fusion.1), kind=kLoop, calls=%fused_computation.18 | loop fusion | flops 18874368 | bytes 9535872 | tf_op jit(solution)/shard_map/convert_element_type | solution.py:29
  8.8 0.2 fusion.80
  9.0 1.9 collective-permute-start
  10.9 5.9 %collective-permute-start.1 = (bf16[3,8,1,96,256]{4,3,2,1,0:T(8,128)(2,1)S(1)}, bf16[3,8,1,96,256]{4,3,2,1,0:T(8,128)(2,1)S(1)}, u32[]{:S(2)}, u32[]{:S(2)}) collective-permute-start(bf16[3,8,1,96,256]{4,3,2,1,0:T(8,128)(2,1)S(1)} %get-tuple-element.6), channel_id=1, source_target_pairs={{1,0},{2,1},{3,2},{4,3},{5,4},{6,5},{7,6},{8,7},{9,8},{10,9},{11,1... | collective-permute-start | bytes 3538952 | tf_op jit(solution)/shard_map/ppermute | solution.py:15
  16.8 0.0 copy-done.3
  16.8 5.0 %fusion.53 = f32[3,8,4,256,96]{3,4,2,1,0:T(8,128)} fusion(bf16[3,8,4,96,256]{4,3,2,1,0:T(8,128)(2,1)S(1)} %fusion.13, bf16[3,3,96,96]{3,2,1,0:T(8,128)(2,1)S(1)} %copy-done.3), kind=kOutput, calls=%fused_computation.67 | convolution fusion | flops 452984832 | bytes 14180352 | tf_op jit(solution)/shard_map/oi,nfyix->nfyox/dot_general | solution.py:36
  21.9 6.7 %collective-permute-done = bf16[3,8,1,96,256]{4,3,2,1,0:T(8,128)(2,1)S(1)} collective-permute-done((bf16[3,8,1,96,256]{4,3,2,1,0:T(8,128)(2,1)S(1)}, bf16[3,8,1,96,256]{4,3,2,1,0:T(8,128)(2,1)S(1)}, u32[]{:S(2)}, u32[]{:S(2)}) %collective-permute-start) | collective-permute-done | bytes 1179680 | tf_op jit(solution)/shard_map/ppermute | solution.py:12
  28.6 1.8 collective-permute-done.1
  30.4 7.1 %fusion.5 = bf16[3,8,6,96,258]{4,3,2,1,0:T(8,128)(2,1)S(1)} fusion(bf16[3,8,1,96,256]{4,3,2,1,0:T(8,128)(2,1)S(1)} %collective-permute-done.1, bf16[3,8,4,96,256]{4,3,2,1,0:T(8,128)(2,1)S(1)} %fusion.13, bf16[3,8,1,96,256]{4,3,2,1,0:T(8,128)(2,1)S(1)} %collective-permute-done), kind=kLoop, calls=%fused_computation.10 | loop fusion | flops 42799104 | bytes 14211072 | tf_op jit(solution)/shard_map/concatenate | solution.py:16
  37.4 0.0 copy-start.1
  37.5 5.4 %fusion.31 = f32[3,8,4,256,96]{3,4,2,1,0:T(8,128)} fusion(bf16[3,8,6,96,258]{4,3,2,1,0:T(8,128)(2,1)S(1)} %fusion.5, bf16[3,3,96,96]{3,2,1,0:T(8,128)(2,1)S(1)} %copy-done.3), kind=kOutput, calls=%fused_computation.43 | convolution fusion | flops 452984832 | bytes 14180352 | tf_op jit(solution)/shard_map/oi,nfyix->nfyox/dot_general | solution.py:36
  42.9 5.2 %fusion.33 = f32[3,8,4,256,96]{3,4,2,1,0:T(8,128)} fusion(bf16[3,8,6,96,258]{4,3,2,1,0:T(8,128)(2,1)S(1)} %fusion.5, bf16[3,3,96,96]{3,2,1,0:T(8,128)(2,1)S(1)} %copy-done.3), kind=kOutput, calls=%fused_computation.45 | convolution fusion | flops 452984832 | bytes 14180352 | tf_op jit(solution)/shard_map/oi,nfyix->nfyox/dot_general | solution.py:36
  48.1 5.1 %fusion.35 = f32[3,8,4,256,96]{3,4,2,1,0:T(8,128)} fusion(bf16[3,8,6,96,258]{4,3,2,1,0:T(8,128)(2,1)S(1)} %fusion.5, bf16[3,3,96,96]{3,2,1,0:T(8,128)(2,1)S(1)} %copy-done.3), kind=kOutput, calls=%fused_computation.47 | convolution fusion | flops 452984832 | bytes 14180352 | tf_op jit(solution)/shard_map/oi,nfyix->nfyox/dot_general | solution.py:36
  53.1 5.1 %fusion.37 = f32[3,8,4,256,96]{3,4,2,1,0:T(8,128)} fusion(bf16[3,8,6,96,258]{4,3,2,1,0:T(8,128)(2,1)S(1)} %fusion.5, bf16[3,3,96,96]{3,2,1,0:T(8,128)(2,1)S(1)} %copy-done.3), kind=kOutput, calls=%fused_computation.49 | convolution fusion | flops 452984832 | bytes 14180352 | tf_op jit(solution)/shard_map/oi,nfyix->nfyox/dot_general | solution.py:36
  58.3 0.0 copy-done.1
  58.3 4.9 %fusion.41 = f32[3,8,4,256,96]{3,4,2,1,0:T(8,128)} fusion(bf16[3,8,6,96,258]{4,3,2,1,0:T(8,128)(2,1)S(1)} %fusion.5, bf16[3,3,96,96]{3,2,1,0:T(8,128)(2,1)S(1)} %copy-done.3), kind=kOutput, calls=%fused_computation.54 | convolution fusion | flops 452984832 | bytes 14180352 | tf_op jit(solution)/shard_map/oi,nfyix->nfyox/dot_general | solution.py:36
  63.2 5.1 %fusion.29 = f32[3,8,4,256,96]{3,4,2,1,0:T(8,128)} fusion(bf16[3,8,1,96,256]{4,3,2,1,0:T(8,128)(2,1)S(1)} %collective-permute-done.1, bf16[3,8,4,96,256]{4,3,2,1,0:T(8,128)(2,1)S(1)} %fusion.13, bf16[3,3,96,96]{3,2,1,0:T(8,128)(2,1)S(1)} %copy-done.3), kind=kOutput, calls=%fused_computation.41 | convolution fusion | flops 462422016 | bytes 15360000 | tf_op jit(solution)/shard_map/oi,nfyix->nfyox/dot_general | solution.py:36
  68.3 4.4 %fusion.39 = f32[3,8,4,256,96]{3,4,2,1,0:T(8,128)} fusion(bf16[3,8,4,96,256]{4,3,2,1,0:T(8,128)(2,1)S(1)} %fusion.13, bf16[3,8,1,96,256]{4,3,2,1,0:T(8,128)(2,1)S(1)} %collective-permute-done, bf16[3,3,96,96]{3,2,1,0:T(8,128)(2,1)S(1)} %copy-done.3), kind=kOutput, calls=%fused_computation.52 | convolution fusion | flops 462422016 | bytes 15360000 | tf_op jit(solution)/shard_map/oi,nfyix->nfyox/dot_general | solution.py:36
  72.7 0.0 copy-start.5
  72.7 31.6 %multiply_reduce_fusion = (f32[3,8,4,256]{3,2,1,0:T(4,128)S(1)}, f32[3,8,4,256,96]{3,4,2,1,0:T(8,128)}) fusion(bf16[3,8,6,96,258]{4,3,2,1,0:T(8,128)(2,1)} %copy-done.1, bf16[3,3,96,96]{3,2,1,0:T(8,128)(2,1)S(1)} %copy-done.3, f32[3,8,4,256,96]{3,4,2,1,0:T(8,128)} %fusion.29, f32[3,8,4,256,96]{3,4,2,1,0:T(8,128)} %fusion.31, ...), kind=kOutput, calls=%fused_computation.26 | convolution fusion | flops 476553216 | bytes 89776128 | tf_op jit(solution)/shard_map/oi,nfyix->nfyox/dot_general | solution.py:36
  104.3 0.0 copy-done.5
  104.4 5.8 %fusion.19 = bf16[3,8,4,96,256]{4,3,2,1,0:T(8,128)(2,1)S(1)} fusion(f32[3,8,4,256,96]{3,4,2,1,0:T(8,128)} %get-tuple-element.10, f32[96]{0:T(128)S(1)} %copy-done.5, f32[3,8,4,256]{3,2,1,0:T(4,128)S(1)} %add_rsqrt_fusion), kind=kLoop, calls=%fused_computation.28 | loop fusion | flops 16515072 | bytes 14254464 | tf_op jit(solution)/shard_map/convert_element_type | solution.py:42
  110.1 0.0 copy-start.2
  110.2 2.2 %copy-done.2 = bf16[3,8,4,96,256]{4,3,2,1,0:T(8,128)(2,1)} copy-done((bf16[3,8,4,96,256]{4,3,2,1,0:T(8,128)(2,1)}, bf16[3,8,4,96,256]{4,3,2,1,0:T(8,128)(2,1)S(1)}, u32[]{:S(2)}) %copy-start.2) | copy-done | bytes 4718616
  112.3 0.0 copy-start.4
  112.3 0.1 slice.133
  112.4 2.7 %stack.2 = bf16[4,3,2,4,96,256]{5,4,3,2,1,0:T(8,128)(2,1)} broadcast(bf16[3,2,4,96,256]{4,3,2,1,0:T(8,128)(2,1)S(1)} %slice.133), dimensions={1,2,3,4,5} | broadcast | bytes 5898240 | tf_op jit(solution)/shard_map/stack | solution.py:47
  115.1 4.9 %all-to-all-start = ((bf16[4,3,2,4,96,256]{5,4,3,2,1,0:T(8,128)(2,1)}), bf16[4,3,2,4,96,256]{5,4,3,2,1,0:T(8,128)(2,1)}, u32[]{:S(2)}, u32[]{:S(2)}) async-start(bf16[4,3,2,4,96,256]{5,4,3,2,1,0:T(8,128)(2,1)} %stack.2), calls=%async_computation | async-start | bytes 9437184 | tf_op jit(solution)/shard_map/all_to_all | solution.py:47
  120.1 0.0 copy-done
  120.1 0.1 constant_dynamic-slice_fusion
  120.2 0.1 iota_compare_fusion.3
  120.3 0.0 copy-done.4
  120.3 7.4 %fusion.45 = f32[3,8,4,256,96]{3,4,2,1,0:T(8,128)} fusion(bf16[3,8,4,96,256]{4,3,2,1,0:T(8,128)(2,1)} %copy-done.2, bf16[3,96,96]{2,1,0:T(8,128)(2,1)S(1)} %copy-done.4), kind=kOutput, calls=%fused_computation.59 | convolution fusion | flops 452984832 | bytes 14180352 | tf_op jit(solution)/shard_map/oi,nfyix->nfyox/dot_general | solution.py:56
  127.6 0.0 slice-start
  127.6 47.1 %all-to-all-done = bf16[4,3,2,4,96,256]{5,4,3,2,1,0:T(8,128)(2,1)} async-done(((bf16[4,3,2,4,96,256]{5,4,3,2,1,0:T(8,128)(2,1)}), bf16[4,3,2,4,96,256]{5,4,3,2,1,0:T(8,128)(2,1)}, u32[]{:S(2)}, u32[]{:S(2)}) %all-to-all-start) | async-done | bytes 4718624 | tf_op jit(solution)/shard_map/all_to_all | solution.py:47
  174.8 0.0 slice-start.1
  174.8 5.4 %fusion.20 = bf16[3,2,4,96,256]{4,0,3,2,1:T(4,128)(2,1)S(1)} fusion(bf16[12,2,4,96,256]{4,3,2,1,0:T(8,128)(2,1)} %bitcast.33, s32[3]{0:T(128)S(1)} %get-tuple-element.8, pred[3]{0:T(512)(128)(4,1)S(1)} %compare_bitcast_fusion), kind=kOutput, calls=%fused_computation.29 | convolution fusion | flops 14155848 | bytes 5898255 | tf_op jit(solution)/shard_map/sk,kfyix->sfyix/dot_general | solution.py:51
  180.2 0.2 copy.27
  180.4 0.0 slice-done
  180.4 0.0 slice-done.1
  180.4 4.4 %fusion.23 = f32[3,8,4,256,96]{3,4,2,1,0:T(8,128)} fusion(bf16[3,2,4,96,256]{4,3,2,1,0:T(8,128)(2,1)S(1)} %copy.27, bf16[3,8,4,96,256]{4,3,2,1,0:T(8,128)(2,1)S(1)} %bitcast.116, bf16[3,96,96]{2,1,0:T(8,128)(2,1)S(1)} %copy-done.4), kind=kOutput, calls=%fused_computation.34 | convolution fusion | flops 462422016 | bytes 15360000 | tf_op jit(solution)/shard_map/oi,nfyix->nfyox/dot_general | solution.py:56
  184.9 11.7 %fusion.15 = bf16[3,8,4,96,256]{4,3,2,1,0:T(8,128)(2,1)} fusion(bf16[3,8,4,96,256]{4,3,2,1,0:T(8,128)(2,1)} %param.6, f32[3,8,4,256,96]{3,4,2,1,0:T(8,128)} %fusion.45, f32[3,8,4,256,96]{3,4,2,1,0:T(8,128)} %fusion.23, pred[3,8]{1,0:T(4,128)(4,1)S(1)} %iota_compare_fusion.3, bf16[3,8,4,96,256]{4,3,2,1,0:T(8,128)(2,1)S(1)} %bitcast.116, ...), kind=kOutput, calls=%fused_computation.20 | convolution fusion | flops 476577792 | bytes 34234880 | tf_op jit(solution)/shard_map/oi,nfyix->nfyox/dot_general | solution.py:56
  (5 shorter events, 0.1 us)
Async XLA Ops:
  0.0 120.1 %copy-start = (s32[12,4]{0,1:T(4,128)S(1)}, s32[12,4]{0,1:T(4,128)}, u32[]{:S(2)}) copy-start(s32[12,4]{0,1:T(4,128)} %param.7) | copy-start | bytes 580
  0.0 16.8 %copy-start.3 = (bf16[3,3,96,96]{3,2,1,0:T(8,128)(2,1)S(1)}, bf16[3,3,96,96]{3,2,1,0:T(8,128)(2,1)}, u32[]{:S(2)}) copy-start(bf16[3,3,96,96]{3,2,1,0:T(8,128)(2,1)} %param.8) | copy-start | bytes 497668
  9.0 19.6 %collective-permute-start = (bf16[3,8,1,96,256]{4,3,2,1,0:T(8,128)(2,1)S(1)}, bf16[3,8,1,96,256]{4,3,2,1,0:T(8,128)(2,1)S(1)}, u32[]{:S(2)}, u32[]{:S(2)}) collective-permute-start(bf16[3,8,1,96,256]{4,3,2,1,0:T(8,128)(2,1)S(1)} %get-tuple-element.5), channel_id=1, source_target_pairs={{0,1},{1,2},{2,3},{3,4},{4,5},{5,6},{6,7},{7,8},{8,9},{9,10},{10,1... | collective-permute-start | bytes 3538952 | tf_op jit(solution)/shard_map/ppermute | solution.py:12
  10.9 19.5 %collective-permute-start.1 = (bf16[3,8,1,96,256]{4,3,2,1,0:T(8,128)(2,1)S(1)}, bf16[3,8,1,96,256]{4,3,2,1,0:T(8,128)(2,1)S(1)}, u32[]{:S(2)}, u32[]{:S(2)}) collective-permute-start(bf16[3,8,1,96,256]{4,3,2,1,0:T(8,128)(2,1)S(1)} %get-tuple-element.6), channel_id=1, source_target_pairs={{1,0},{2,1},{3,2},{4,3},{5,4},{6,5},{7,6},{8,7},{9,8},{10,9},{11,1... | collective-permute-start | bytes 3538952 | tf_op jit(solution)/shard_map/ppermute | solution.py:15
  37.4 20.8 %copy-start.1 = (bf16[3,8,6,96,258]{4,3,2,1,0:T(8,128)(2,1)}, bf16[3,8,6,96,258]{4,3,2,1,0:T(8,128)(2,1)S(1)}, u32[]{:S(2)}) copy-start(bf16[3,8,6,96,258]{4,3,2,1,0:T(8,128)(2,1)S(1)} %fusion.5) | copy-start | bytes 21399556
  72.7 31.6 %copy-start.5 = (f32[96]{0:T(128)S(1)}, f32[96]{0:T(128)}, u32[]{:S(2)}) copy-start(f32[96]{0:T(128)} %param.11) | copy-start | bytes 1156
  110.1 2.2 %copy-start.2 = (bf16[3,8,4,96,256]{4,3,2,1,0:T(8,128)(2,1)}, bf16[3,8,4,96,256]{4,3,2,1,0:T(8,128)(2,1)S(1)}, u32[]{:S(2)}) copy-start(bf16[3,8,4,96,256]{4,3,2,1,0:T(8,128)(2,1)S(1)} %fusion.19) | copy-start | bytes 14155780
  112.3 7.9 %copy-start.4 = (bf16[3,96,96]{2,1,0:T(8,128)(2,1)S(1)}, bf16[3,96,96]{2,1,0:T(8,128)(2,1)}, u32[]{:S(2)}) copy-start(bf16[3,96,96]{2,1,0:T(8,128)(2,1)} %param.9) | copy-start | bytes 165892
  115.1 59.6 %all-to-all-start = ((bf16[4,3,2,4,96,256]{5,4,3,2,1,0:T(8,128)(2,1)}), bf16[4,3,2,4,96,256]{5,4,3,2,1,0:T(8,128)(2,1)}, u32[]{:S(2)}, u32[]{:S(2)}) async-start(bf16[4,3,2,4,96,256]{5,4,3,2,1,0:T(8,128)(2,1)} %stack.2), calls=%async_computation | async-start | bytes 9437184 | tf_op jit(solution)/shard_map/all_to_all | solution.py:47
  127.6 52.8 %slice-start = ((s8[4718592]{0:T(1024)(128)(4,1)}), s8[524288]{0:T(1024)(128)(4,1)S(1)}, s32[]{:S(2)}) async-start(s8[4718592]{0:T(1024)(128)(4,1)} %bitcast.115), calls=%async_computation.1 | async-start | bytes 1048576
  174.8 5.6 %slice-start.1 = ((s8[4718592]{0:T(1024)(128)(4,1)}), s8[4194304]{0:T(1024)(128)(4,1)S(1)}, s32[]{:S(2)}) async-start(s8[4718592]{0:T(1024)(128)(4,1)} %bitcast.115), calls=%async_computation.2 | async-start | bytes 8388608
